TPU v7x, 32 devices: a whole 2x2x4 slice. The times are simulated.
32 devices in a mesh: row: 8 (over y, x, core), col: 4 (over z).
Axes of the slice: x: 2, y: 2, z: 4, core: 2. Of those that a mesh axis runs over, the one named last changes fastest.
Arguments:
- tokens: bfloat16 [32768, 768], P(('row', 'col')), may hold values from -6 to 6
- segment: int32 [32, 1024], replicated, may hold values from 0 to 63, never falling along the last dimension, each value on 1 to 512 neighbouring positions
- w_qkv: bfloat16 [768, 2304], P('row', 'col'), may hold values from -0.21875 to 0.21875
- w_out: bfloat16 [768, 768], P('row', 'col'), may hold values from -0.875 to 0.875
- w_up: bfloat16 [768, 3072], P('row', 'col'), may hold values from -0.21875 to 0.21875
- w_down: bfloat16 [3072, 768], P('row', 'col'), may hold values from -0.109375 to 0.109375
- bias_query: float32 [768], replicated, may hold values from -3 to 3
- bias_value: float32 [768], replicated, may hold values from -3 to 3
- bias_out: float32 [768], replicated, may hold values from -3 to 3
- gain_attn: float32 [768], replicated, may hold values from 0.25 to 1.75
- shift_attn: float32 [768], replicated, may hold values from -3 to 3
- bias_up: float32 [3072], replicated, may hold values from -3 to 3
- bias_down: float32 [768], replicated, may hold values from -3 to 3
- gain_ffn: float32 [768], replicated, may hold values from 0.25 to 1.75
- shift_ffn: float32 [768], replicated, may hold values from -3 to 3
- cotangent: bfloat16 [32768, 768], P(('row', 'col')), may hold values from -6 to 6
Outputs:
- layer_out: bfloat16 [32768, 768], P(('row', 'col'))
- grad_tokens: float32 [32768, 768], P(('row', 'col'))
- grad_qkv: float32 [768, 2304], P('row', 'col')
- grad_out: float32 [768, 768], P('row', 'col')
- grad_up: float32 [768, 3072], P('row', 'col')
- grad_down: float32 [3072, 768], P('row', 'col')
- grad_bias_query: float32 [768], replicated
- grad_bias_value: float32 [768], replicated
- grad_bias_out: float32 [768], replicated
- grad_gain_attn: float32 [768], replicated
- grad_shift_attn: float32 [768], replicated
- grad_bias_up: float32 [3072], replicated
- grad_bias_down: float32 [768], replicated
- grad_gain_ffn: float32 [768], replicated
- grad_shift_ffn: float32 [768], replicated
Inputs may be any that keep to these rules, and one draw needn't show every extreme that they name: `segment`: within each packed sequence the document numbers never fall; a document is a run of equal numbers, and some document has 512 tokens.
All inputs are finite; a program needn't handle non-finite values.
Results may differ from a plain program's by a relative error of at most 0.019.
Values may be sent and summed in bfloat16 or wider, within the bound.
A program may use at most 192 MiB of HBM per device.

v0:
```python
import jax
import jax.numpy as jnp
from jax import lax
from jax.sharding import PartitionSpec as P

HEADS = 12
HEAD_DIM = 64
LEN = 1024
norm_eps = 1e-05
masked_score = -1e30


def gather_block(blocks):
    widened = (
        lax.all_gather(blocks[0], "col", axis=1, tiled=True),
        lax.all_gather(blocks[1], "col", axis=1, tiled=True),
    )
    return (
        lax.all_gather(widened[0], "row", axis=0, tiled=True),
        lax.all_gather(widened[1], "row", axis=0, tiled=True),
    )


def reduce_grads(grads):
    narrowed = (
        lax.psum_scatter(
            grads[0].astype(jnp.bfloat16), "col", scatter_dimension=1, tiled=True
        ).astype(jnp.float32),
        lax.psum_scatter(
            grads[1].astype(jnp.bfloat16), "col", scatter_dimension=1, tiled=True
        ).astype(jnp.float32),
    )
    return (
        lax.psum_scatter(
            narrowed[0].astype(jnp.bfloat16), "row", scatter_dimension=0, tiled=True
        ).astype(jnp.float32),
        lax.psum_scatter(
            narrowed[1].astype(jnp.bfloat16), "row", scatter_dimension=0, tiled=True
        ).astype(jnp.float32),
    )


def dot_rows(left, right):
    return lax.dot_general(
        left, right, (((0,), (0,)), ((), ())), preferred_element_type=jnp.float32
    )


def dot_back(left, right):
    return lax.dot_general(
        left, right, (((1,), (1,)), ((), ())), preferred_element_type=jnp.float32
    )


def norm_rows(resid, gain, shift):
    centre = resid - jnp.mean(resid, axis=1, keepdims=True)
    factor = lax.rsqrt(jnp.mean(centre * centre, axis=1, keepdims=True) + norm_eps)
    normed = centre * factor
    return (normed * gain + shift, normed, factor)


def norm_back(grad_result, normed, factor, gain):
    grad_normed = grad_result * gain
    grad_resid = factor * (
        grad_normed
        - jnp.mean(grad_normed, axis=1, keepdims=True)
        - normed * jnp.mean(grad_normed * normed, axis=1, keepdims=True)
    )
    return (grad_resid, jnp.sum(grad_result * normed, axis=0), jnp.sum(grad_result, axis=0))


def gelu_exact(value):
    return jax.nn.gelu(value, approximate=False)


def pair_scores(query_part, key_part, seg_query, seg_key):
    query_heads = query_part.reshape(query_part.shape[0], 2, HEAD_DIM)
    key_heads = key_part.reshape(key_part.shape[0], 2, HEAD_DIM)
    raw = jnp.einsum("qhd,khd->hqk", query_heads, key_heads, preferred_element_type=jnp.float32)
    same = seg_query[:, None] == seg_key[None, :]
    return jnp.where(same[None], raw * HEAD_DIM ** (-0.5), masked_score)


def per_device(
    tokens,
    segment,
    w_qkv,
    w_out,
    w_up,
    w_down,
    bias_query,
    bias_value,
    bias_out,
    gain_attn,
    shift_attn,
    bias_up,
    bias_down,
    gain_ffn,
    shift_ffn,
    cotangent,
):
    model = tokens.shape[1]
    tok_rows = tokens.shape[0]
    pairs = HEADS // 2
    width = 2 * HEAD_DIM
    qlen = min(tok_rows, LEN)
    local_seqs = tok_rows // qlen
    item_count = local_seqs * pairs
    device_at = lax.axis_index("row") * lax.axis_size("col") + lax.axis_index("col")
    seq_first = device_at * tok_rows // LEN
    attn_qkv, attn_out = gather_block((w_qkv, w_out))
    ffn_up, ffn_down = gather_block((w_up, w_down))
    projected = jnp.dot(tokens, attn_qkv, preferred_element_type=jnp.float32)
    queries = (projected[:, :model] + bias_query).astype(jnp.bfloat16)
    keys_values = jnp.concatenate(
        [projected[:, model : 2 * model], projected[:, 2 * model :] + bias_value], axis=1
    ).astype(jnp.bfloat16)

    def item_place(item):
        seq_at = item // pairs
        pair_at = item % pairs
        return (seq_at, seq_at * qlen, seq_at * LEN, pair_at * width)

    def item_segments(seq_at):
        segrow = lax.dynamic_index_in_dim(segment, seq_first + seq_at, 0, keepdims=False)
        return (segrow, segrow)

    def attend_step(item, carried):
        context, logsum = carried
        seq_at, query_row, key_row, start_col = item_place(item)
        query_part = lax.dynamic_slice(queries, (query_row, start_col), (qlen, width))
        key_part = lax.dynamic_slice(keys_values, (key_row, start_col), (LEN, width))
        value_part = lax.dynamic_slice(keys_values, (key_row, model + start_col), (LEN, width))
        seg_query, seg_key = item_segments(seq_at)
        scores = pair_scores(query_part, key_part, seg_query, seg_key)
        peak = jnp.max(scores, axis=2, keepdims=True)
        expo = jnp.exp(scores - peak)
        total = jnp.sum(expo, axis=2, keepdims=True)
        prob = (expo / total).astype(jnp.bfloat16)
        result = jnp.einsum(
            "hqk,khd->qhd",
            prob,
            value_part.reshape(LEN, 2, HEAD_DIM),
            preferred_element_type=jnp.float32,
        )
        context = lax.dynamic_update_slice(
            context, result.reshape(qlen, width).astype(jnp.bfloat16), (query_row, start_col)
        )
        logsum = lax.dynamic_update_slice(
            logsum, (peak + jnp.log(total))[None, :, :, 0], (item, 0, 0)
        )
        return (context, logsum)

    context, logsum = lax.fori_loop(
        0,
        item_count,
        attend_step,
        (jnp.zeros((tok_rows, model), jnp.bfloat16), jnp.zeros((item_count, 2, qlen), jnp.float32)),
    )
    attended = jnp.dot(context, attn_out, preferred_element_type=jnp.float32) + bias_out
    hidden, normed_one, factor_one = norm_rows(
        tokens.astype(jnp.float32) + attended, gain_attn, shift_attn
    )
    hidden_low = hidden.astype(jnp.bfloat16)
    upward = jnp.dot(hidden_low, ffn_up, preferred_element_type=jnp.float32) + bias_up
    active_low = gelu_exact(upward).astype(jnp.bfloat16)
    ffn_result = jnp.dot(active_low, ffn_down, preferred_element_type=jnp.float32) + bias_down
    output, normed_two, factor_two = norm_rows(hidden + ffn_result, gain_ffn, shift_ffn)
    grad_two, grad_gain_ffn, grad_shift_ffn = norm_back(
        cotangent.astype(jnp.float32), normed_two, factor_two, gain_ffn
    )
    grad_bias_down = jnp.sum(grad_two, axis=0)
    grad_two_low = grad_two.astype(jnp.bfloat16)
    grad_down_full = dot_rows(active_low, grad_two_low)
    grad_active = dot_back(grad_two_low, ffn_down)
    grad_upward = jax.vjp(gelu_exact, upward)[1](grad_active)[0]
    grad_bias_up = jnp.sum(grad_upward, axis=0)
    grad_up_low = grad_upward.astype(jnp.bfloat16)
    grad_up_full = dot_rows(hidden_low, grad_up_low)
    grad_hidden = grad_two + dot_back(grad_up_low, ffn_up)
    block_up, block_down = reduce_grads((grad_up_full, grad_down_full))
    grad_one, grad_gain_attn, grad_shift_attn = norm_back(
        grad_hidden, normed_one, factor_one, gain_attn
    )
    grad_bias_out = jnp.sum(grad_one, axis=0)
    grad_one_low = grad_one.astype(jnp.bfloat16)
    grad_out_full = dot_rows(context, grad_one_low)
    grad_context = dot_back(grad_one_low, attn_out).astype(jnp.bfloat16)

    def back_step(item, carried):
        grad_queries, grad_kv = carried
        seq_at, query_row, key_row, start_col = item_place(item)
        query_part = lax.dynamic_slice(queries, (query_row, start_col), (qlen, width))
        key_part = lax.dynamic_slice(keys_values, (key_row, start_col), (LEN, width))
        value_part = lax.dynamic_slice(keys_values, (key_row, model + start_col), (LEN, width))
        grad_part = lax.dynamic_slice(grad_context, (query_row, start_col), (qlen, width))
        seg_query, seg_key = item_segments(seq_at)
        lse_now = lax.dynamic_index_in_dim(logsum, item, 0, keepdims=False)
        scores = pair_scores(query_part, key_part, seg_query, seg_key)
        prob = jnp.exp(scores - lse_now[:, :, None])
        grad_heads = grad_part.reshape(qlen, 2, HEAD_DIM)
        value_heads = value_part.reshape(LEN, 2, HEAD_DIM)
        grad_prob = jnp.einsum(
            "qhd,khd->hqk", grad_heads, value_heads, preferred_element_type=jnp.float32
        )
        grad_value = jnp.einsum(
            "hqk,qhd->khd",
            prob.astype(jnp.bfloat16),
            grad_heads,
            preferred_element_type=jnp.float32,
        )
        inner = jnp.sum(prob * grad_prob, axis=2, keepdims=True)
        grad_raw = (prob * (grad_prob - inner) * HEAD_DIM ** (-0.5)).astype(jnp.bfloat16)
        grad_query = jnp.einsum(
            "hqk,khd->qhd",
            grad_raw,
            key_part.reshape(LEN, 2, HEAD_DIM),
            preferred_element_type=jnp.float32,
        )
        grad_key = jnp.einsum(
            "hqk,qhd->khd",
            grad_raw,
            query_part.reshape(qlen, 2, HEAD_DIM),
            preferred_element_type=jnp.float32,
        )
        grad_queries = lax.dynamic_update_slice(
            grad_queries, grad_query.reshape(qlen, width), (query_row, start_col)
        )
        grad_kv = lax.dynamic_update_slice(
            grad_kv, grad_key.reshape(LEN, width), (key_row, start_col)
        )
        grad_kv = lax.dynamic_update_slice(
            grad_kv, grad_value.reshape(LEN, width), (key_row, model + start_col)
        )
        return (grad_queries, grad_kv)

    grad_queries, grad_kv_whole = lax.fori_loop(
        0,
        item_count,
        back_step,
        (
            jnp.zeros((tok_rows, model), jnp.float32),
            jnp.zeros((keys_values.shape[0], 2 * model), jnp.float32),
        ),
    )
    grad_kv = grad_kv_whole
    grad_bias_query = jnp.sum(grad_queries, axis=0)
    grad_bias_value = jnp.sum(grad_kv[:, model:], axis=0)
    grad_proj_low = jnp.concatenate([grad_queries, grad_kv], axis=1).astype(jnp.bfloat16)
    grad_qkv_full = dot_rows(tokens, grad_proj_low)
    grad_tokens = grad_one + dot_back(grad_proj_low, attn_qkv)
    block_qkv, block_out = reduce_grads((grad_qkv_full, grad_out_full))
    (
        sum_query,
        sum_value,
        sum_out,
        sum_gain_attn,
        sum_shift_attn,
        sum_up,
        sum_down,
        sum_gain_ffn,
        sum_shift_ffn,
    ) = lax.psum(
        (
            grad_bias_query,
            grad_bias_value,
            grad_bias_out,
            grad_gain_attn,
            grad_shift_attn,
            grad_bias_up,
            grad_bias_down,
            grad_gain_ffn,
            grad_shift_ffn,
        ),
        ("row", "col"),
    )
    return (
        output.astype(jnp.bfloat16),
        grad_tokens,
        block_qkv,
        block_out,
        block_up,
        block_down,
        sum_query,
        sum_value,
        sum_out,
        sum_gain_attn,
        sum_shift_attn,
        sum_up,
        sum_down,
        sum_gain_ffn,
        sum_shift_ffn,
    )


def solution(mesh):
    return jax.shard_map(
        per_device,
        mesh=mesh,
        in_specs=(
            P(("row", "col"), None),
            P(),
            P("row", "col"),
            P("row", "col"),
            P("row", "col"),
            P("row", "col"),
            P(),
            P(),
            P(),
            P(),
            P(),
            P(),
            P(),
            P(),
            P(),
            P(("row", "col"), None),
        ),
        out_specs=(
            P(("row", "col"), None),
            P(("row", "col"), None),
            P("row", "col"),
            P("row", "col"),
            P("row", "col"),
            P("row", "col"),
            P(),
            P(),
            P(),
            P(),
            P(),
            P(),
            P(),
            P(),
            P(),
        ),
        check_vma=False,
    )
```

profile of v0, /device:TPU:0, one launch (start us, length us, event | category | flops | bytes accessed | tf_op | source)
XLA Modules:
  0.0 1040.2 jit_solution(14863380718797404151)
XLA Ops:
  7.2 17.5 %all-gather = bf16[4,576,96]{1,2,0:T(8,128)(2,1)S(1)} all-gather(bf16[1,576,96]{1,2,0:T(8,128)(2,1)} %bitcast.129), channel_id=1, replica_groups=mesh['row'=8,'col'=4] {'col'}, dimensions={0}, use_global_device_ids=true | all-gather | bytes 552960 | tf_op jit(solution)/shard_map/all_gather | solution.py:15
  27.1 14.3 %all_gather.26 = bf16[96,768]{0,1:T(8,128)(2,1)S(1)} all-gather(bf16[96,192]{0,1:T(8,128)(2,1)S(1)} %copy.96), channel_id=1, replica_groups=mesh['row'=8,'col'=4] {'col'}, dimensions={1}, use_global_device_ids=true | all-gather | bytes 184320 | tf_op jit(solution)/shard_map/all_gather | solution.py:16
  42.3 18.1 %all_gather.28 = bf16[96,3072]{1,0:T(8,128)(2,1)} all-gather(bf16[96,768]{1,0:T(8,128)(2,1)} %param.24), channel_id=1, replica_groups=mesh['row'=8,'col'=4] {'col'}, dimensions={1}, use_global_device_ids=true | all-gather | bytes 737280 | tf_op jit(solution)/shard_map/all_gather | solution.py:15
  60.5 15.7 %all_gather.30 = bf16[384,768]{0,1:T(8,128)(2,1)} all-gather(bf16[384,192]{0,1:T(8,128)(2,1)S(1)} %copy-done.12), channel_id=1, replica_groups=mesh['row'=8,'col'=4] {'col'}, dimensions={1}, use_global_device_ids=true | all-gather | bytes 737280 | tf_op jit(solution)/shard_map/all_gather | solution.py:16
  80.5 6.5 fusion.93
  89.3 2.9 copy.94
  95.2 60.3 %while.34 = (s32[]{:T(128)}, bf16[1024,768]{0,1:T(8,128)(2,1)}, f32[6,2,1024]{2,1,0:T(2,128)S(1)}, bf16[1024,1536]{0,1:T(8,128)(2,1)}, s32[]{:T(128)}, /*index=5...) while((s32[]{:T(128)}, bf16[1024,768]{0,1:T(8,128)(2,1)}, ...), condition=%wide.region_3.4_spmd, body=%wide.region_0.3_spmd.sunk | while | flops 563214336 | bytes 32584120 | solution.py:154
  101.7 2.8 fusion.146
  121.7 2.8 fusion.146
  131.7 2.8 fusion.146
  141.8 2.8 fusion.146
  156.7 3.8 fusion.88
  161.1 38.2 %multiply_convert_fusion.1 = (bf16[1024,3072]{1,0:T(8,128)(2,1)}, f32[1024,3072]{1,0:T(8,128)}, f32[1024,3072]{1,0:T(8,128)}) fusion(f32[3072]{0:T(1024)S(1)} %copy-done.23, bf16[768,3072]{1,0:T(8,128)(2,1)} %all-gather.10.cloned.1.call-done, f32[1024,768]{0,1:T(8,128)S(1)} %get-tuple-element.618, f32[768]{0:T(1024)S(1)} %copy-done.26, ...), kind=kOutput, calls=%fused_computation.55 | convolution fusion | flops 5043388416 | bytes 39348224 | tf_op jit(solution)/shard_map/dot_general | solution.py:165
  199.3 9.7 fusion.89
  211.2 19.2 %fusion.90 = (f32[3072]{0:T(1024)}, bf16[1024,3072]{1,0:T(8,128)(2,1)}) fusion(f32[1024,3072]{1,0:T(8,128)} %get-tuple-element.602, bf16[3072,768]{0,1:T(8,128)(2,1)} %all-gather.12.cloned.1.call-done, f32[1024]{0:T(1024)S(1)} %get-tuple-element.625, f32[1024,768]{0,1:T(8,128)S(1)} %get-tuple-element.621, f32[1024]{0:T(1024)S(1)} %broadcast_multiply_fusion.4, ...), kind=kOutput, calls=%fused_computation.132 | convolution fusion | flops 4889244672 | bytes 40938496 | tf_op jit(solution)/shard_map/dot_general | solution.py:50
  230.4 11.6 %multiply_reduce_fusion.1 = (f32[768]{0:T(1024)}, f32[1024]{0:T(1024)S(1)}, f32[1024]{0:T(1024)S(1)}, f32[768]{0:T(1024)}, f32[1024,768]{0,1:T(8,128)S(1)}) fusion(f32[1024,768]{0,1:T(8,128)} %copy-done.3, f32[1024]{0:T(1024)S(1)} %add_rsqrt_fusion.1, f32[1024]{0:T(1024)S(1)} %broadcast_multiply_fusion.5, f32[768]{0:T(1024)S(1)} %copy-done.19, ...), kind=kOutput, calls=%fused_computation.90 | convolution fusion | flops 4845989888 | bytes 22065152 | tf_op jit(solution)/shard_map/dot_general | solution.py:50
  245.4 3.9 convolution_convert_fusion.4
  249.3 4.8 convolution_convert_fusion.3
  254.1 3.5 broadcast_in_dim.122
  259.6 356.7 %while.35 = (s32[]{:T(128)}, f32[1024,768]{0,1:T(8,128)}, f32[1024,1536]{0,1:T(8,128)}, bf16[1024,1536]{0,1:T(8,128)(2,1)}, s32[]{:T(128)}, /*index=5*/s32[32,10...) while((s32[]{:T(128)}, f32[1024,768]{0,1:T(8,128)}, ...), condition=%wide.region_14.15_spmd, body=%wide.region_12.14_spmd.sunk | while | flops 1397757952 | bytes 74240520 | solution.py:237
  265.1 5.5 fusion.157
  272.3 4.5 fusion.158
  279.9 15.0 %fusion.160 = f32[2,64,1024]{2,1,0:T(8,128)} fusion(bf16[1024,2,64]{0,2,1:T(8,128)(2,1)S(1)} %bitcast.113, f32[2,1024,1024]{1,2,0:T(8,128)} %fusion.157, f32[2,1024,1024]{1,2,0:T(8,128)} %fusion.158, f32[2,1024]{1,0:T(2,128)S(1)} %dynamic-slice_bitcast_fusion.2, pred[1024,1024]{0,1:T(8,128)(4,1)} %broadcast_compare_fusion.5), kind=kOutput, calls=%fused_computation.23.clone.1 | convolution fusion | flops 291507200 | bytes 18620416 | tf_op jit(solution)/shard_map/while/body/eval_jaxpr/hqk,khd->qhd/dot_general | solution.py:214
  294.9 15.2 %fusion.159 = f32[2,64,1024]{2,1,0:T(8,128)} fusion(bf16[1024,2,64]{0,2,1:T(8,128)(2,1)} %bitcast.115, f32[2,1024,1024]{1,2,0:T(8,128)} %fusion.157, f32[2,1024,1024]{1,2,0:T(8,128)} %fusion.158, f32[2,1024]{1,0:T(2,128)S(1)} %dynamic-slice_bitcast_fusion.2, pred[1024,1024]{0,1:T(8,128)(4,1)} %broadcast_compare_fusion.5), kind=kOutput, calls=%fused_computation.22.clone.1 | convolution fusion | flops 291507200 | bytes 18620416 | tf_op jit(solution)/shard_map/while/body/eval_jaxpr/hqk,qhd->khd/dot_general | solution.py:220
  312.3 6.0 fusion.161
  324.4 5.5 fusion.157
  331.6 4.5 fusion.158
  339.2 15.0 %fusion.160 = f32[2,64,1024]{2,1,0:T(8,128)} fusion(bf16[1024,2,64]{0,2,1:T(8,128)(2,1)S(1)} %bitcast.113, f32[2,1024,1024]{1,2,0:T(8,128)} %fusion.157, f32[2,1024,1024]{1,2,0:T(8,128)} %fusion.158, f32[2,1024]{1,0:T(2,128)S(1)} %dynamic-slice_bitcast_fusion.2, pred[1024,1024]{0,1:T(8,128)(4,1)} %broadcast_compare_fusion.5), kind=kOutput, calls=%fused_computation.23.clone.1 | convolution fusion | flops 291507200 | bytes 18620416 | tf_op jit(solution)/shard_map/while/body/eval_jaxpr/hqk,khd->qhd/dot_general | solution.py:214
  354.2 15.2 %fusion.159 = f32[2,64,1024]{2,1,0:T(8,128)} fusion(bf16[1024,2,64]{0,2,1:T(8,128)(2,1)} %bitcast.115, f32[2,1024,1024]{1,2,0:T(8,128)} %fusion.157, f32[2,1024,1024]{1,2,0:T(8,128)} %fusion.158, f32[2,1024]{1,0:T(2,128)S(1)} %dynamic-slice_bitcast_fusion.2, pred[1024,1024]{0,1:T(8,128)(4,1)} %broadcast_compare_fusion.5), kind=kOutput, calls=%fused_computation.22.clone.1 | convolution fusion | flops 291507200 | bytes 18620416 | tf_op jit(solution)/shard_map/while/body/eval_jaxpr/hqk,qhd->khd/dot_general | solution.py:220
  371.7 6.0 fusion.161
  383.8 5.5 fusion.157
  391.0 4.5 fusion.158
  398.6 15.0 %fusion.160 = f32[2,64,1024]{2,1,0:T(8,128)} fusion(bf16[1024,2,64]{0,2,1:T(8,128)(2,1)S(1)} %bitcast.113, f32[2,1024,1024]{1,2,0:T(8,128)} %fusion.157, f32[2,1024,1024]{1,2,0:T(8,128)} %fusion.158, f32[2,1024]{1,0:T(2,128)S(1)} %dynamic-slice_bitcast_fusion.2, pred[1024,1024]{0,1:T(8,128)(4,1)} %broadcast_compare_fusion.5), kind=kOutput, calls=%fused_computation.23.clone.1 | convolution fusion | flops 291507200 | bytes 18620416 | tf_op jit(solution)/shard_map/while/body/eval_jaxpr/hqk,khd->qhd/dot_general | solution.py:214
  413.6 15.2 %fusion.159 = f32[2,64,1024]{2,1,0:T(8,128)} fusion(bf16[1024,2,64]{0,2,1:T(8,128)(2,1)} %bitcast.115, f32[2,1024,1024]{1,2,0:T(8,128)} %fusion.157, f32[2,1024,1024]{1,2,0:T(8,128)} %fusion.158, f32[2,1024]{1,0:T(2,128)S(1)} %dynamic-slice_bitcast_fusion.2, pred[1024,1024]{0,1:T(8,128)(4,1)} %broadcast_compare_fusion.5), kind=kOutput, calls=%fused_computation.22.clone.1 | convolution fusion | flops 291507200 | bytes 18620416 | tf_op jit(solution)/shard_map/while/body/eval_jaxpr/hqk,qhd->khd/dot_general | solution.py:220
  431.1 6.0 fusion.161
  443.2 5.5 fusion.157
  450.4 4.5 fusion.158
  458.0 15.0 %fusion.160 = f32[2,64,1024]{2,1,0:T(8,128)} fusion(bf16[1024,2,64]{0,2,1:T(8,128)(2,1)S(1)} %bitcast.113, f32[2,1024,1024]{1,2,0:T(8,128)} %fusion.157, f32[2,1024,1024]{1,2,0:T(8,128)} %fusion.158, f32[2,1024]{1,0:T(2,128)S(1)} %dynamic-slice_bitcast_fusion.2, pred[1024,1024]{0,1:T(8,128)(4,1)} %broadcast_compare_fusion.5), kind=kOutput, calls=%fused_computation.23.clone.1 | convolution fusion | flops 291507200 | bytes 18620416 | tf_op jit(solution)/shard_map/while/body/eval_jaxpr/hqk,khd->qhd/dot_general | solution.py:214
  473.0 15.2 %fusion.159 = f32[2,64,1024]{2,1,0:T(8,128)} fusion(bf16[1024,2,64]{0,2,1:T(8,128)(2,1)} %bitcast.115, f32[2,1024,1024]{1,2,0:T(8,128)} %fusion.157, f32[2,1024,1024]{1,2,0:T(8,128)} %fusion.158, f32[2,1024]{1,0:T(2,128)S(1)} %dynamic-slice_bitcast_fusion.2, pred[1024,1024]{0,1:T(8,128)(4,1)} %broadcast_compare_fusion.5), kind=kOutput, calls=%fused_computation.22.clone.1 | convolution fusion | flops 291507200 | bytes 18620416 | tf_op jit(solution)/shard_map/while/body/eval_jaxpr/hqk,qhd->khd/dot_general | solution.py:220
  490.5 6.0 fusion.161
  502.6 5.5 fusion.157
  509.8 4.5 fusion.158
  517.4 15.0 %fusion.160 = f32[2,64,1024]{2,1,0:T(8,128)} fusion(bf16[1024,2,64]{0,2,1:T(8,128)(2,1)S(1)} %bitcast.113, f32[2,1024,1024]{1,2,0:T(8,128)} %fusion.157, f32[2,1024,1024]{1,2,0:T(8,128)} %fusion.158, f32[2,1024]{1,0:T(2,128)S(1)} %dynamic-slice_bitcast_fusion.2, pred[1024,1024]{0,1:T(8,128)(4,1)} %broadcast_compare_fusion.5), kind=kOutput, calls=%fused_computation.23.clone.1 | convolution fusion | flops 291507200 | bytes 18620416 | tf_op jit(solution)/shard_map/while/body/eval_jaxpr/hqk,khd->qhd/dot_general | solution.py:214
  532.4 15.2 %fusion.159 = f32[2,64,1024]{2,1,0:T(8,128)} fusion(bf16[1024,2,64]{0,2,1:T(8,128)(2,1)} %bitcast.115, f32[2,1024,1024]{1,2,0:T(8,128)} %fusion.157, f32[2,1024,1024]{1,2,0:T(8,128)} %fusion.158, f32[2,1024]{1,0:T(2,128)S(1)} %dynamic-slice_bitcast_fusion.2, pred[1024,1024]{0,1:T(8,128)(4,1)} %broadcast_compare_fusion.5), kind=kOutput, calls=%fused_computation.22.clone.1 | convolution fusion | flops 291507200 | bytes 18620416 | tf_op jit(solution)/shard_map/while/body/eval_jaxpr/hqk,qhd->khd/dot_general | solution.py:220
  549.9 6.0 fusion.161
  562.0 5.5 fusion.157
  569.2 4.5 fusion.158
  576.8 15.0 %fusion.160 = f32[2,64,1024]{2,1,0:T(8,128)} fusion(bf16[1024,2,64]{0,2,1:T(8,128)(2,1)S(1)} %bitcast.113, f32[2,1024,1024]{1,2,0:T(8,128)} %fusion.157, f32[2,1024,1024]{1,2,0:T(8,128)} %fusion.158, f32[2,1024]{1,0:T(2,128)S(1)} %dynamic-slice_bitcast_fusion.2, pred[1024,1024]{0,1:T(8,128)(4,1)} %broadcast_compare_fusion.5), kind=kOutput, calls=%fused_computation.23.clone.1 | convolution fusion | flops 291507200 | bytes 18620416 | tf_op jit(solution)/shard_map/while/body/eval_jaxpr/hqk,khd->qhd/dot_general | solution.py:214
  591.7 15.2 %fusion.159 = f32[2,64,1024]{2,1,0:T(8,128)} fusion(bf16[1024,2,64]{0,2,1:T(8,128)(2,1)} %bitcast.115, f32[2,1024,1024]{1,2,0:T(8,128)} %fusion.157, f32[2,1024,1024]{1,2,0:T(8,128)} %fusion.158, f32[2,1024]{1,0:T(2,128)S(1)} %dynamic-slice_bitcast_fusion.2, pred[1024,1024]{0,1:T(8,128)(4,1)} %broadcast_compare_fusion.5), kind=kOutput, calls=%fused_computation.22.clone.1 | convolution fusion | flops 291507200 | bytes 18620416 | tf_op jit(solution)/shard_map/while/body/eval_jaxpr/hqk,qhd->khd/dot_general | solution.py:220
  609.2 6.0 fusion.161
  616.4 3.4 convert.16
  622.5 6.5 fusion.54
  629.1 9.6 convolution_convert_fusion
  639.4 9.8 convolution_convert_fusion.1
  651.3 46.1 %reduce-scatter.15.cloned.1.call-done = bf16[768,576]{0,1:T(8,128)(2,1)} async-done(((bf16[768,2304]{0,1:T(8,128)(2,1)}), bf16[768,576]{0,1:T(8,128)(2,1)}) %reduce-scatter.15.cloned.1.call-update) | async-done | bytes 884752 | tf_op jit(solution)/shard_map/reduce_scatter | solution.py:26
  699.6 85.5 %reduce-scatter.23.cloned.1.call-done = bf16[3072,192]{0,1:T(8,128)(2,1)} async-done(((bf16[3072,768]{0,1:T(8,128)(2,1)}), bf16[3072,192]{0,1:T(8,128)(2,1)}) %reduce-scatter.23.cloned.1.call-update) | async-done | bytes 1179664 | tf_op jit(solution)/shard_map/reduce_scatter | solution.py:29
  787.7 85.6 %reduce-scatter.19.cloned.1.call-done = bf16[768,768]{1,0:T(8,128)(2,1)} async-done(((bf16[768,3072]{1,0:T(8,128)(2,1)}), bf16[768,768]{1,0:T(8,128)(2,1)}) %reduce-scatter.19.cloned.1.call-update) | async-done | bytes 1179664 | tf_op jit(solution)/shard_map/reduce_scatter | solution.py:26
  873.3 9.8 fusion.69
  883.1 3.8 copy.106
  886.9 4.1 fusion.61
  895.8 42.1 %all-reduce = (f32[768]{0:T(1024)}, f32[768]{0:T(1024)}, f32[768]{0:T(1024)}, f32[768]{0:T(1024)}, f32[768]{0:T(1024)}, /*index=5*/f32[3072]{0:T(1024)}, f32[768]{0:T(1024)}, f32[768]{0:T(1024)}, f32[768]{0:T(1024)}) all-reduce(f32[768]{0:T(1024)S(1)} %get-tuple-element.615, ...), channel_id=1, replica_groups=mesh['row'=8,'col'=4] {'row','col'}, use_global_device_ids=true, to_apply=%region_24.25 | all-reduce | flops 9216 | bytes 73728 | tf_op jit(solution)/shard_map/psum | solution.py:263
  939.6 10.1 reduce-scatter.25.cloned.1.call-done
  951.6 39.7 %reduce-scatter.29.cloned.1.call-done = bf16[384,192]{1,0:T(8,128)(2,1)} async-done(((bf16[3072,192]{1,0:T(8,128)(2,1)}), bf16[384,192]{1,0:T(8,128)(2,1)}) %reduce-scatter.29.cloned.1.call-update) | async-done | bytes 147472
  993.2 38.0 %reduce-scatter.21.cloned.1.call-done = bf16[96,768]{1,0:T(8,128)(2,1)} async-done(((bf16[768,768]{1,0:T(8,128)(2,1)}), bf16[96,768]{1,0:T(8,128)(2,1)}) %reduce-scatter.21.cloned.1.call-update) | async-done | bytes 147472 | tf_op jit(solution)/shard_map/reduce_scatter | solution.py:34
  (241 shorter events, 171.3 us)
Async XLA Ops:
  7.2 53.3 %copy-start.12 = (bf16[384,192]{0,1:T(8,128)(2,1)S(1)}, bf16[384,192]{0,1:T(8,128)(2,1)}, u32[]{:S(2)}) copy-start(bf16[384,192]{0,1:T(8,128)(2,1)} %param.25) | copy-start | bytes 442372
  7.2 73.3 %all-gather.6.cloned.1.call-start = ((), (), s32[]{:S(2)}) async-start(), calls=%async_computation.8 | async-start | bytes 3981312 | tf_op jit(solution)/shard_map/all_gather | solution.py:19
  24.9 54.0 %copy-start.9 = (bf16[1024,768]{1,0:T(8,128)(2,1)S(1)}, bf16[1024,768]{1,0:T(8,128)(2,1)}, u32[]{:S(2)}) copy-start(bf16[1024,768]{1,0:T(8,128)(2,1)} %param.35) | copy-start | bytes 4718596
  26.2 129.4 %all-gather.8.cloned.1.call-start = ((), (), s32[]{:S(2)}) async-start(), calls=%async_computation.9 | async-start | bytes 1327104 | tf_op jit(solution)/shard_map/all_gather | solution.py:20
  42.2 118.9 %all-gather.10.cloned.1.call-start = ((), (), s32[]{:S(2)}) async-start(), calls=%async_computation.10 | async-start | bytes 5308416 | tf_op jit(solution)/shard_map/all_gather | solution.py:19
  60.4 138.9 %all-gather.12.cloned.1.call-start = ((), (), s32[]{:S(2)}) async-start(), calls=%async_computation.11 | async-start | bytes 5308416 | tf_op jit(solution)/shard_map/all_gather | solution.py:20
  76.2 573.0 %reduce-scatter.17.cloned.1.call-start = ((), (), s32[]{:S(2)}) async-start(), calls=%async_computation.13 | async-start | bytes 1474560 | tf_op jit(solution)/shard_map/reduce_scatter | solution.py:29
  80.5 6.7 copy-start.17
  80.5 6.7 copy-start.18
  95.2 61.6 %copy-start.24 = (f32[768]{0:T(1024)S(1)}, f32[768]{0:T(1024)}, u32[]{:S(2)}) copy-start(f32[768]{0:T(1024)} %param.28) | copy-start | bytes 9220
  155.5 1.2 copy-start.6
  155.5 5.1 copy-start.13
  156.7 4.3 copy-start.19
  156.7 4.3 copy-start.23
  156.7 4.3 copy-start.26
  160.6 38.7 %copy-start.3 = (f32[1024,768]{0,1:T(8,128)}, f32[1024,768]{0,1:T(8,128)S(1)}, u32[]{:S(2)}) copy-start(f32[1024,768]{0,1:T(8,128)S(1)} %get-tuple-element.618) | copy-start | bytes 9437188
  161.0 38.3 %copy-start.25 = (f32[768]{0:T(1024)S(1)}, f32[768]{0:T(1024)}, u32[]{:S(2)}) copy-start(f32[768]{0:T(1024)} %param.32) | copy-start | bytes 9220
  199.3 10.2 copy-start.15
  209.0 1.4 copy-start.2
  230.4 11.6 %copy-start.4 = (f32[1024,768]{0,1:T(8,128)S(1)}, f32[1024,768]{0,1:T(8,128)}, u32[]{:S(2)}) copy-start(f32[1024,768]{0,1:T(8,128)} %copy-done.3) | copy-start | bytes 9437188
  243.7 1.6 copy-start.7
  249.2 448.1 %reduce-scatter.15.cloned.1.call-start = ((), (), s32[]{:S(2)}) async-start(), calls=%async_computation.12 | async-start | bytes 4423680 | tf_op jit(solution)/shard_map/reduce_scatter | solution.py:26
  271.6 0.7 copy-start
  294.9 17.5 %copy-start.1 = (bf16[1024,128]{0,1:T(8,128)(2,1)S(1)}, bf16[1024,128]{0,1:T(8,128)(2,1)}, u32[]{:S(2)}) copy-start(bf16[1024,128]{0,1:T(8,128)(2,1)} %copy.124) | copy-start | bytes 786436 | tf_op jit(solution)/shard_map/while
  330.9 0.7 copy-start
  354.2 17.5 %copy-start.1 = (bf16[1024,128]{0,1:T(8,128)(2,1)S(1)}, bf16[1024,128]{0,1:T(8,128)(2,1)}, u32[]{:S(2)}) copy-start(bf16[1024,128]{0,1:T(8,128)(2,1)} %copy.124) | copy-start | bytes 786436 | tf_op jit(solution)/shard_map/while
  390.3 0.7 copy-start
  413.6 17.5 %copy-start.1 = (bf16[1024,128]{0,1:T(8,128)(2,1)S(1)}, bf16[1024,128]{0,1:T(8,128)(2,1)}, u32[]{:S(2)}) copy-start(bf16[1024,128]{0,1:T(8,128)(2,1)} %copy.124) | copy-start | bytes 786436 | tf_op jit(solution)/shard_map/while
  449.7 0.7 copy-start
  473.0 17.5 %copy-start.1 = (bf16[1024,128]{0,1:T(8,128)(2,1)S(1)}, bf16[1024,128]{0,1:T(8,128)(2,1)}, u32[]{:S(2)}) copy-start(bf16[1024,128]{0,1:T(8,128)(2,1)} %copy.124) | copy-start | bytes 786436 | tf_op jit(solution)/shard_map/while
  509.1 0.7 copy-start
  532.4 17.5 %copy-start.1 = (bf16[1024,128]{0,1:T(8,128)(2,1)S(1)}, bf16[1024,128]{0,1:T(8,128)(2,1)}, u32[]{:S(2)}) copy-start(bf16[1024,128]{0,1:T(8,128)(2,1)} %copy.124) | copy-start | bytes 786436 | tf_op jit(solution)/shard_map/while
  568.5 0.7 copy-start
  591.7 17.5 %copy-start.1 = (bf16[1024,128]{0,1:T(8,128)(2,1)S(1)}, bf16[1024,128]{0,1:T(8,128)(2,1)}, u32[]{:S(2)}) copy-start(bf16[1024,128]{0,1:T(8,128)(2,1)} %copy.124) | copy-start | bytes 786436 | tf_op jit(solution)/shard_map/while
  616.4 3.7 copy-start.5
  619.8 1.7 copy-start.8
  619.8 2.6 copy-start.10
  620.5 1.5 copy-start.11
  629.0 156.1 %reduce-scatter.23.cloned.1.call-start = ((), (), s32[]{:S(2)}) async-start(), calls=%async_computation.16 | async-start | bytes 5898240 | tf_op jit(solution)/shard_map/reduce_scatter | solution.py:29
  638.7 0.7 copy-start.27
  638.7 234.5 %reduce-scatter.19.cloned.1.call-start = ((), (), s32[]{:S(2)}) async-start(), calls=%async_computation.14 | async-start | bytes 5898240 | tf_op jit(solution)/shard_map/reduce_scatter | solution.py:26
  649.2 288.7 %reduce-scatter.27.cloned.1.call-start = ((), (), s32[]{:S(2)}) async-start(), calls=%async_computation.18 | async-start | bytes 442368
  651.2 298.5 %reduce-scatter.25.cloned.1.call-start = ((), (), s32[]{:S(2)}) async-start(), calls=%async_computation.17 | async-start | bytes 1105920
  699.6 291.8 %reduce-scatter.29.cloned.1.call-start = ((), (), s32[]{:S(2)}) async-start(), calls=%async_computation.19 | async-start | bytes 1769472
  787.6 243.5 %reduce-scatter.21.cloned.1.call-start = ((), (), s32[]{:S(2)}) async-start(), calls=%async_computation.15 | async-start | bytes 1327104 | tf_op jit(solution)/shard_map/reduce_scatter | solution.py:34
  883.1 3.8 copy-start.22
  891.1 4.7 copy-start.14
  891.1 4.8 copy-start.16
  891.1 4.8 copy-start.20
  891.1 4.8 copy-start.21
Sparse Core Ops, SparseCore 0:
  26.3 35.5 all-gather.5
  64.4 23.9 all-gather.7
  90.2 38.7 all-gather.9
  130.7 39.6 all-gather.11
  249.4 30.9 reduce-scatter.16
  629.1 68.1 reduce-scatter.14
  699.6 85.4 reduce-scatter.22
  787.4 85.7 reduce-scatter.18
  876.3 34.3 reduce-scatter.26
  913.8 35.9 reduce-scatter.24
  953.0 38.2 reduce-scatter.28
  994.5 36.6 reduce-scatter.20
where the time goes:
time: 1050 us; the launch traced here: 1040 us
  matrix products  439 us (42%)
  waiting for transfers between devices  305 us (29%)
  local copies, waits for them, and re-layouts  128 us (12%)
  blocking collectives  108 us (10%)
  other arithmetic  43.5 us (4%)
  between operations  15.1 us (1%)
    reduce_scatter x2, waiting for transfers between devices, reduce_grads(): lax.psum_scatter(grads[0].astype(jnp.bfloat16), 'col', scatter_dimension=...  132 us
    dot_general x6, matrix products, back_step(): jnp.einsum('hqk,qhd->khd', grad_raw, query_part.reshape(qlen, 2, HEAD_DIM...  91.2 us
    dot_general x6, matrix products, back_step(): jnp.einsum('hqk,khd->qhd', grad_raw, key_part.reshape(LEN, 2, HEAD_DIM),...  89.8 us
    reduce_scatter x2, waiting for transfers between devices, reduce_grads(): lax.psum_scatter(grads[1].astype(jnp.bfloat16), 'col', scatter_dimension=...  85.5 us
    unnamed x15, waiting for transfers between devices  50.1 us
    dot_general x4, matrix products, dot_back(): lax.dot_general(left, right, (((1,), (1,)), ((), ())), preferred_element_...  45.4 us
    psum x1, blocking collectives, per_device(): lax.psum((grad_bias_query, grad_bias_value, grad_bias_out, grad_gain_attn...  42.1 us
    dot_general x12, matrix products, pair_scores(): jnp.einsum('qhd,khd->hqk', query_heads, key_heads, preferred_element_type...  38.5 us
  transfers between devices with their start and end apart: 12, of which 6 were waited for; matrix products, arithmetic and copies ran while one was open for 53% of the time, Pallas kernels for 0%

commit v1 on v0

--- a/solution.py
+++ b/solution.py
@@ -10,10 +10,31 @@
 masked_score = -1e30
 
 
+def in_order(pieces, dim):
+    dims = list(pieces.shape[1:])
+    dims[dim] *= pieces.shape[0]
+    return jnp.moveaxis(pieces, 0, dim).reshape(dims)
+
+
+def doubled(shard, axis):
+    length, position = (lax.axis_size(axis), lax.axis_index(axis))
+    blocks, bit = (shard[None], 1)
+    while bit < length:
+        theirs = lax.ppermute(blocks, axis, [(i, i ^ bit) for i in range(length)])
+        low = position & bit == 0
+        blocks = jnp.concatenate([jnp.where(low, blocks, theirs), jnp.where(low, theirs, blocks)])
+        bit *= 2
+    return blocks
+
+
+def gather_by_bits(x, axis, dim):
+    return in_order(doubled(x, axis), dim)
+
+
 def gather_block(blocks):
     widened = (
         lax.all_gather(blocks[0], "col", axis=1, tiled=True),
-        lax.all_gather(blocks[1], "col", axis=1, tiled=True),
+        gather_by_bits(blocks[1], "col", 1),
     )
     return (
         lax.all_gather(widened[0], "row", axis=0, tiled=True),

time: 1050 us -> 1040 us (level)
  blocking collectives: 108 us -> 78.6 us
  waiting for transfers between devices: 305 us -> 322 us
    all_gather x2 -> x0, blocking collectives: 30 us -> none  [gather_block(): lax.all_gather(blocks[1], 'col', axis=1, tiled=True)]
    ppermute x0 -> x4, waiting for transfers between devices: none -> 19.2 us  [doubled(): theirs = lax.ppermute(blocks, axis, [(i, i ^ bit) for i in range(length)])]
    unnamed x66 -> x67, local copies, waits for them, and re-layouts: 30.7 us -> 28.8 us
  transfers between devices with their start and end apart: 12 -> 16, of which waited for: 6 -> 10; matrix products, arithmetic and copies ran while one was open for 53% -> 53% of each run, Pallas kernels for 0% -> 0%
where the time goes in v1:
time: 1040 us
  matrix products  439 us (42%)
  waiting for transfers between devices  322 us (31%)
  local copies, waits for them, and re-layouts  126 us (12%)
  blocking collectives  78.6 us (8%)
  other arithmetic  49 us (5%)
  between operations  15.1 us (1%)
    reduce_scatter x2, waiting for transfers between devices, reduce_grads(): lax.psum_scatter(grads[0].astype(jnp.bfloat16), 'col', scatter_dimension=...  129 us
    dot_general x6, matrix products, back_step(): jnp.einsum('hqk,qhd->khd', grad_raw, query_part.reshape(qlen, 2, HEAD_DIM...  91 us
    dot_general x6, matrix products, back_step(): jnp.einsum('hqk,khd->qhd', grad_raw, key_part.reshape(LEN, 2, HEAD_DIM),...  89.8 us
    reduce_scatter x2, waiting for transfers between devices, reduce_grads(): lax.psum_scatter(grads[1].astype(jnp.bfloat16), 'col', scatter_dimension=...  85.5 us
    unnamed x15, waiting for transfers between devices  50.1 us
    dot_general x4, matrix products, dot_back(): lax.dot_general(left, right, (((1,), (1,)), ((), ())), preferred_element_...  45.4 us
    psum x1, blocking collectives, per_device(): lax.psum((grad_bias_query, grad_bias_value, grad_bias_out, grad_gain_attn...  42.1 us
    dot_general x12, matrix products, pair_scores(): jnp.einsum('qhd,khd->hqk', query_heads, key_heads, preferred_element_type...  38.4 us
  transfers between devices with their start and end apart: 16, of which 10 were waited for; matrix products, arithmetic and copies ran while one was open for 53% of the time, Pallas kernels for 0%

profile of v1, /device:TPU:0, one launch (start us, length us, event | category | flops | bytes accessed | tf_op | source)
XLA Modules:
  0.0 1037.9 jit_solution(4045979018817789024)
XLA Ops:
  7.2 17.5 %all-gather = bf16[4,576,96]{1,2,0:T(8,128)(2,1)S(1)} all-gather(bf16[1,576,96]{1,2,0:T(8,128)(2,1)} %bitcast.142), channel_id=1, replica_groups=mesh['row'=8,'col'=4] {'col'}, dimensions={0}, use_global_device_ids=true | all-gather | bytes 552960 | tf_op jit(solution)/shard_map/all_gather | solution.py:36
  34.5 2.9 collective-permute-done.1
  39.5 19.1 %all_gather.21 = bf16[96,3072]{1,0:T(8,128)(2,1)} all-gather(bf16[96,768]{1,0:T(8,128)(2,1)S(1)} %copy-done.13), channel_id=1, replica_groups=mesh['row'=8,'col'=4] {'col'}, dimensions={1}, use_global_device_ids=true | all-gather | bytes 737280 | tf_op jit(solution)/shard_map/all_gather | solution.py:36
  60.2 6.9 collective-permute-done.2
  72.1 6.9 collective-permute-done.3
  81.3 5.8 fusion.93
  89.4 2.9 copy.75
  95.3 60.2 %while.34 = (s32[]{:T(128)}, bf16[1024,768]{0,1:T(8,128)(2,1)}, f32[6,2,1024]{2,1,0:T(2,128)S(1)}, bf16[1024,1536]{0,1:T(8,128)(2,1)}, s32[]{:T(128)}, /*index=5...) while((s32[]{:T(128)}, bf16[1024,768]{0,1:T(8,128)(2,1)}, ...), condition=%wide.region_3.4_spmd, body=%wide.region_0.3_spmd.sunk | while | flops 563214336 | bytes 32584120 | solution.py:175
  101.8 2.8 fusion.146
  121.8 2.8 fusion.146
  131.9 2.8 fusion.146
  156.7 3.8 fusion.88
  161.0 38.3 %multiply_convert_fusion.1 = (bf16[1024,3072]{1,0:T(8,128)(2,1)}, f32[1024,3072]{1,0:T(8,128)}, f32[1024,3072]{1,0:T(8,128)}) fusion(f32[3072]{0:T(1024)S(1)} %copy-done.24, bf16[768,3072]{1,0:T(8,128)(2,1)} %all-gather.10.cloned.1.call-done, f32[1024,768]{0,1:T(8,128)S(1)} %get-tuple-element.595, f32[768]{0:T(1024)S(1)} %copy-done.27, ...), kind=kOutput, calls=%fused_computation.55 | convolution fusion | flops 5043388416 | bytes 39348224 | tf_op jit(solution)/shard_map/dot_general | solution.py:186
  199.3 9.8 fusion.89
  211.3 19.2 %fusion.90 = (f32[3072]{0:T(1024)}, bf16[1024,3072]{1,0:T(8,128)(2,1)}) fusion(f32[1024,3072]{1,0:T(8,128)} %get-tuple-element.571, bf16[3072,768]{0,1:T(8,128)(2,1)} %all-gather.12.cloned.1.call-done, f32[1024]{0:T(1024)S(1)} %get-tuple-element.602, f32[1024,768]{0,1:T(8,128)S(1)} %get-tuple-element.598, f32[1024]{0:T(1024)S(1)} %broadcast_multiply_fusion.4, ...), kind=kOutput, calls=%fused_computation.144 | convolution fusion | flops 4889244672 | bytes 40938496 | tf_op jit(solution)/shard_map/dot_general | solution.py:71
  230.5 11.6 %multiply_reduce_fusion.1 = (f32[768]{0:T(1024)}, f32[1024]{0:T(1024)S(1)}, f32[1024]{0:T(1024)S(1)}, f32[768]{0:T(1024)}, f32[1024,768]{0,1:T(8,128)S(1)}) fusion(f32[1024,768]{0,1:T(8,128)} %copy-done.3, f32[1024]{0:T(1024)S(1)} %add_rsqrt_fusion.1, f32[1024]{0:T(1024)S(1)} %broadcast_multiply_fusion.5, f32[768]{0:T(1024)S(1)} %copy-done.20, ...), kind=kOutput, calls=%fused_computation.90 | convolution fusion | flops 4845989888 | bytes 22065152 | tf_op jit(solution)/shard_map/dot_general | solution.py:71
  245.4 3.8 convolution_convert_fusion.4
  249.3 4.8 convolution_convert_fusion.3
  254.2 3.4 broadcast_in_dim.130
  259.7 356.5 %while.35 = (s32[]{:T(128)}, f32[1024,768]{0,1:T(8,128)}, f32[1024,1536]{0,1:T(8,128)}, bf16[1024,1536]{0,1:T(8,128)(2,1)}, s32[]{:T(128)}, /*index=5*/s32[32,10...) while((s32[]{:T(128)}, f32[1024,768]{0,1:T(8,128)}, ...), condition=%wide.region_14.15_spmd, body=%wide.region_12.14_spmd.sunk | while | flops 1397757952 | bytes 74240520 | solution.py:258
  265.1 5.5 fusion.157
  272.4 4.5 fusion.158
  279.9 15.0 %fusion.160 = f32[2,64,1024]{2,1,0:T(8,128)} fusion(bf16[1024,2,64]{0,2,1:T(8,128)(2,1)S(1)} %bitcast.124, f32[2,1024,1024]{1,2,0:T(8,128)} %fusion.157, f32[2,1024,1024]{1,2,0:T(8,128)} %fusion.158, f32[2,1024]{1,0:T(2,128)S(1)} %dynamic-slice_bitcast_fusion.2, pred[1024,1024]{0,1:T(8,128)(4,1)} %broadcast_compare_fusion.5), kind=kOutput, calls=%fused_computation.23.clone.1 | convolution fusion | flops 291507200 | bytes 18620416 | tf_op jit(solution)/shard_map/while/body/eval_jaxpr/hqk,khd->qhd/dot_general | solution.py:235
  294.9 15.2 %fusion.159 = f32[2,64,1024]{2,1,0:T(8,128)} fusion(bf16[1024,2,64]{0,2,1:T(8,128)(2,1)} %bitcast.126, f32[2,1024,1024]{1,2,0:T(8,128)} %fusion.157, f32[2,1024,1024]{1,2,0:T(8,128)} %fusion.158, f32[2,1024]{1,0:T(2,128)S(1)} %dynamic-slice_bitcast_fusion.2, pred[1024,1024]{0,1:T(8,128)(4,1)} %broadcast_compare_fusion.5), kind=kOutput, calls=%fused_computation.22.clone.1 | convolution fusion | flops 291507200 | bytes 18620416 | tf_op jit(solution)/shard_map/while/body/eval_jaxpr/hqk,qhd->khd/dot_general | solution.py:241
  312.4 6.0 fusion.161
  324.4 5.5 fusion.157
  331.7 4.5 fusion.158
  339.3 15.0 %fusion.160 = f32[2,64,1024]{2,1,0:T(8,128)} fusion(bf16[1024,2,64]{0,2,1:T(8,128)(2,1)S(1)} %bitcast.124, f32[2,1024,1024]{1,2,0:T(8,128)} %fusion.157, f32[2,1024,1024]{1,2,0:T(8,128)} %fusion.158, f32[2,1024]{1,0:T(2,128)S(1)} %dynamic-slice_bitcast_fusion.2, pred[1024,1024]{0,1:T(8,128)(4,1)} %broadcast_compare_fusion.5), kind=kOutput, calls=%fused_computation.23.clone.1 | convolution fusion | flops 291507200 | bytes 18620416 | tf_op jit(solution)/shard_map/while/body/eval_jaxpr/hqk,khd->qhd/dot_general | solution.py:235
  354.2 15.2 %fusion.159 = f32[2,64,1024]{2,1,0:T(8,128)} fusion(bf16[1024,2,64]{0,2,1:T(8,128)(2,1)} %bitcast.126, f32[2,1024,1024]{1,2,0:T(8,128)} %fusion.157, f32[2,1024,1024]{1,2,0:T(8,128)} %fusion.158, f32[2,1024]{1,0:T(2,128)S(1)} %dynamic-slice_bitcast_fusion.2, pred[1024,1024]{0,1:T(8,128)(4,1)} %broadcast_compare_fusion.5), kind=kOutput, calls=%fused_computation.22.clone.1 | convolution fusion | flops 291507200 | bytes 18620416 | tf_op jit(solution)/shard_map/while/body/eval_jaxpr/hqk,qhd->khd/dot_general | solution.py:241
  371.7 6.0 fusion.161
  383.8 5.5 fusion.157
  391.0 4.5 fusion.158
  398.6 15.0 %fusion.160 = f32[2,64,1024]{2,1,0:T(8,128)} fusion(bf16[1024,2,64]{0,2,1:T(8,128)(2,1)S(1)} %bitcast.124, f32[2,1024,1024]{1,2,0:T(8,128)} %fusion.157, f32[2,1024,1024]{1,2,0:T(8,128)} %fusion.158, f32[2,1024]{1,0:T(2,128)S(1)} %dynamic-slice_bitcast_fusion.2, pred[1024,1024]{0,1:T(8,128)(4,1)} %broadcast_compare_fusion.5), kind=kOutput, calls=%fused_computation.23.clone.1 | convolution fusion | flops 291507200 | bytes 18620416 | tf_op jit(solution)/shard_map/while/body/eval_jaxpr/hqk,khd->qhd/dot_general | solution.py:235
  413.6 15.2 %fusion.159 = f32[2,64,1024]{2,1,0:T(8,128)} fusion(bf16[1024,2,64]{0,2,1:T(8,128)(2,1)} %bitcast.126, f32[2,1024,1024]{1,2,0:T(8,128)} %fusion.157, f32[2,1024,1024]{1,2,0:T(8,128)} %fusion.158, f32[2,1024]{1,0:T(2,128)S(1)} %dynamic-slice_bitcast_fusion.2, pred[1024,1024]{0,1:T(8,128)(4,1)} %broadcast_compare_fusion.5), kind=kOutput, calls=%fused_computation.22.clone.1 | convolution fusion | flops 291507200 | bytes 18620416 | tf_op jit(solution)/shard_map/while/body/eval_jaxpr/hqk,qhd->khd/dot_general | solution.py:241
  431.1 6.0 fusion.161
  443.2 5.5 fusion.157
  450.4 4.5 fusion.158
  458.0 15.0 %fusion.160 = f32[2,64,1024]{2,1,0:T(8,128)} fusion(bf16[1024,2,64]{0,2,1:T(8,128)(2,1)S(1)} %bitcast.124, f32[2,1024,1024]{1,2,0:T(8,128)} %fusion.157, f32[2,1024,1024]{1,2,0:T(8,128)} %fusion.158, f32[2,1024]{1,0:T(2,128)S(1)} %dynamic-slice_bitcast_fusion.2, pred[1024,1024]{0,1:T(8,128)(4,1)} %broadcast_compare_fusion.5), kind=kOutput, calls=%fused_computation.23.clone.1 | convolution fusion | flops 291507200 | bytes 18620416 | tf_op jit(solution)/shard_map/while/body/eval_jaxpr/hqk,khd->qhd/dot_general | solution.py:235
  472.9 15.2 %fusion.159 = f32[2,64,1024]{2,1,0:T(8,128)} fusion(bf16[1024,2,64]{0,2,1:T(8,128)(2,1)} %bitcast.126, f32[2,1024,1024]{1,2,0:T(8,128)} %fusion.157, f32[2,1024,1024]{1,2,0:T(8,128)} %fusion.158, f32[2,1024]{1,0:T(2,128)S(1)} %dynamic-slice_bitcast_fusion.2, pred[1024,1024]{0,1:T(8,128)(4,1)} %broadcast_compare_fusion.5), kind=kOutput, calls=%fused_computation.22.clone.1 | convolution fusion | flops 291507200 | bytes 18620416 | tf_op jit(solution)/shard_map/while/body/eval_jaxpr/hqk,qhd->khd/dot_general | solution.py:241
  490.4 6.0 fusion.161
  502.5 5.5 fusion.157
  509.7 4.5 fusion.158
  517.3 15.0 %fusion.160 = f32[2,64,1024]{2,1,0:T(8,128)} fusion(bf16[1024,2,64]{0,2,1:T(8,128)(2,1)S(1)} %bitcast.124, f32[2,1024,1024]{1,2,0:T(8,128)} %fusion.157, f32[2,1024,1024]{1,2,0:T(8,128)} %fusion.158, f32[2,1024]{1,0:T(2,128)S(1)} %dynamic-slice_bitcast_fusion.2, pred[1024,1024]{0,1:T(8,128)(4,1)} %broadcast_compare_fusion.5), kind=kOutput, calls=%fused_computation.23.clone.1 | convolution fusion | flops 291507200 | bytes 18620416 | tf_op jit(solution)/shard_map/while/body/eval_jaxpr/hqk,khd->qhd/dot_general | solution.py:235
  532.3 15.2 %fusion.159 = f32[2,64,1024]{2,1,0:T(8,128)} fusion(bf16[1024,2,64]{0,2,1:T(8,128)(2,1)} %bitcast.126, f32[2,1024,1024]{1,2,0:T(8,128)} %fusion.157, f32[2,1024,1024]{1,2,0:T(8,128)} %fusion.158, f32[2,1024]{1,0:T(2,128)S(1)} %dynamic-slice_bitcast_fusion.2, pred[1024,1024]{0,1:T(8,128)(4,1)} %broadcast_compare_fusion.5), kind=kOutput, calls=%fused_computation.22.clone.1 | convolution fusion | flops 291507200 | bytes 18620416 | tf_op jit(solution)/shard_map/while/body/eval_jaxpr/hqk,qhd->khd/dot_general | solution.py:241
  549.7 6.0 fusion.161
  561.9 5.5 fusion.157
  569.1 4.5 fusion.158
  576.7 15.0 %fusion.160 = f32[2,64,1024]{2,1,0:T(8,128)} fusion(bf16[1024,2,64]{0,2,1:T(8,128)(2,1)S(1)} %bitcast.124, f32[2,1024,1024]{1,2,0:T(8,128)} %fusion.157, f32[2,1024,1024]{1,2,0:T(8,128)} %fusion.158, f32[2,1024]{1,0:T(2,128)S(1)} %dynamic-slice_bitcast_fusion.2, pred[1024,1024]{0,1:T(8,128)(4,1)} %broadcast_compare_fusion.5), kind=kOutput, calls=%fused_computation.23.clone.1 | convolution fusion | flops 291507200 | bytes 18620416 | tf_op jit(solution)/shard_map/while/body/eval_jaxpr/hqk,khd->qhd/dot_general | solution.py:235
  591.6 15.2 %fusion.159 = f32[2,64,1024]{2,1,0:T(8,128)} fusion(bf16[1024,2,64]{0,2,1:T(8,128)(2,1)} %bitcast.126, f32[2,1024,1024]{1,2,0:T(8,128)} %fusion.157, f32[2,1024,1024]{1,2,0:T(8,128)} %fusion.158, f32[2,1024]{1,0:T(2,128)S(1)} %dynamic-slice_bitcast_fusion.2, pred[1024,1024]{0,1:T(8,128)(4,1)} %broadcast_compare_fusion.5), kind=kOutput, calls=%fused_computation.22.clone.1 | convolution fusion | flops 291507200 | bytes 18620416 | tf_op jit(solution)/shard_map/while/body/eval_jaxpr/hqk,qhd->khd/dot_general | solution.py:241
  609.1 6.0 fusion.161
  616.2 3.4 convert.16
  622.3 6.5 fusion.54
  628.9 9.6 convolution_convert_fusion
  639.2 9.8 convolution_convert_fusion.1
  651.1 43.9 %reduce-scatter.15.cloned.1.call-done = bf16[768,576]{0,1:T(8,128)(2,1)} async-done(((bf16[768,2304]{0,1:T(8,128)(2,1)}), bf16[768,576]{0,1:T(8,128)(2,1)}) %reduce-scatter.15.cloned.1.call-update) | async-done | bytes 884752 | tf_op jit(solution)/shard_map/reduce_scatter | solution.py:47
  697.3 85.5 %reduce-scatter.23.cloned.1.call-done = bf16[3072,192]{0,1:T(8,128)(2,1)} async-done(((bf16[3072,768]{0,1:T(8,128)(2,1)}), bf16[3072,192]{0,1:T(8,128)(2,1)}) %reduce-scatter.23.cloned.1.call-update) | async-done | bytes 1179664 | tf_op jit(solution)/shard_map/reduce_scatter | solution.py:50
  785.3 85.6 %reduce-scatter.19.cloned.1.call-done = bf16[768,768]{1,0:T(8,128)(2,1)} async-done(((bf16[768,3072]{1,0:T(8,128)(2,1)}), bf16[768,768]{1,0:T(8,128)(2,1)}) %reduce-scatter.19.cloned.1.call-update) | async-done | bytes 1179664 | tf_op jit(solution)/shard_map/reduce_scatter | solution.py:47
  870.9 9.8 fusion.69
  880.8 3.8 copy.86
  884.6 4.1 fusion.61
  893.5 42.1 %all-reduce = (f32[768]{0:T(1024)}, f32[768]{0:T(1024)}, f32[768]{0:T(1024)}, f32[768]{0:T(1024)}, f32[768]{0:T(1024)}, /*index=5*/f32[3072]{0:T(1024)}, f32[768]{0:T(1024)}, f32[768]{0:T(1024)}, f32[768]{0:T(1024)}) all-reduce(f32[768]{0:T(1024)S(1)} %get-tuple-element.584, ...), channel_id=1, replica_groups=mesh['row'=8,'col'=4] {'row','col'}, use_global_device_ids=true, to_apply=%region_24.25 | all-reduce | flops 9216 | bytes 73728 | tf_op jit(solution)/shard_map/psum | solution.py:284
  937.3 10.1 reduce-scatter.25.cloned.1.call-done
  949.3 39.8 %reduce-scatter.29.cloned.1.call-done = bf16[384,192]{1,0:T(8,128)(2,1)} async-done(((bf16[3072,192]{1,0:T(8,128)(2,1)}), bf16[384,192]{1,0:T(8,128)(2,1)}) %reduce-scatter.29.cloned.1.call-update) | async-done | bytes 147472
  990.9 38.0 %reduce-scatter.21.cloned.1.call-done = bf16[96,768]{1,0:T(8,128)(2,1)} async-done(((bf16[768,768]{1,0:T(8,128)(2,1)}), bf16[96,768]{1,0:T(8,128)(2,1)}) %reduce-scatter.21.cloned.1.call-update) | async-done | bytes 147472 | tf_op jit(solution)/shard_map/reduce_scatter | solution.py:55
  (257 shorter events, 187.2 us)
Async XLA Ops:
  7.2 32.3 %copy-start.13 = (bf16[96,768]{1,0:T(8,128)(2,1)S(1)}, bf16[96,768]{1,0:T(8,128)(2,1)}, u32[]{:S(2)}) copy-start(bf16[96,768]{1,0:T(8,128)(2,1)} %param.24) | copy-start | bytes 442372
  7.2 61.7 %copy-start.10 = (bf16[1024,768]{1,0:T(8,128)(2,1)S(1)}, bf16[1024,768]{1,0:T(8,128)(2,1)}, u32[]{:S(2)}) copy-start(bf16[1024,768]{1,0:T(8,128)(2,1)} %param.20) | copy-start | bytes 4718596
  7.2 74.1 %all-gather.6.cloned.1.call-start = ((), (), s32[]{:S(2)}) async-start(), calls=%async_computation.8 | async-start | bytes 3981312 | tf_op jit(solution)/shard_map/all_gather | solution.py:40
  26.1 44.4 %copy-start.9 = (bf16[1024,768]{1,0:T(8,128)(2,1)S(1)}, bf16[1024,768]{1,0:T(8,128)(2,1)}, u32[]{:S(2)}) copy-start(bf16[1024,768]{1,0:T(8,128)(2,1)} %param.35) | copy-start | bytes 4718596
  26.2 129.3 %all-gather.8.cloned.1.call-start = ((), (), s32[]{:S(2)}) async-start(), calls=%async_computation.9 | async-start | bytes 1327104 | tf_op jit(solution)/shard_map/all_gather | solution.py:41
  26.2 4.7 collective-permute-start
  31.7 5.7 collective-permute-start.1
  39.4 121.6 %all-gather.10.cloned.1.call-start = ((), (), s32[]{:S(2)}) async-start(), calls=%async_computation.10 | async-start | bytes 5308416 | tf_op jit(solution)/shard_map/all_gather | solution.py:40
  58.6 140.7 %all-gather.12.cloned.1.call-start = ((), (), s32[]{:S(2)}) async-start(), calls=%async_computation.11 | async-start | bytes 5308416 | tf_op jit(solution)/shard_map/all_gather | solution.py:41
  58.6 8.5 collective-permute-start.2
  68.8 10.2 collective-permute-start.3
  81.0 6.3 copy-start.18
  81.0 6.3 copy-start.19
  81.0 568.1 %reduce-scatter.17.cloned.1.call-start = ((), (), s32[]{:S(2)}) async-start(), calls=%async_computation.13 | async-start | bytes 1474560 | tf_op jit(solution)/shard_map/reduce_scatter | solution.py:50
  95.3 61.4 %copy-start.25 = (f32[768]{0:T(1024)S(1)}, f32[768]{0:T(1024)}, u32[]{:S(2)}) copy-start(f32[768]{0:T(1024)} %param.28) | copy-start | bytes 9220
  155.5 1.2 copy-start.6
  155.5 5.1 copy-start.14
  156.6 4.3 copy-start.20
  156.6 4.3 copy-start.24
  156.7 4.3 copy-start.27
  160.5 38.7 %copy-start.3 = (f32[1024,768]{0,1:T(8,128)}, f32[1024,768]{0,1:T(8,128)S(1)}, u32[]{:S(2)}) copy-start(f32[1024,768]{0,1:T(8,128)S(1)} %get-tuple-element.595) | copy-start | bytes 9437188
  160.9 38.3 %copy-start.26 = (f32[768]{0:T(1024)S(1)}, f32[768]{0:T(1024)}, u32[]{:S(2)}) copy-start(f32[768]{0:T(1024)} %param.32) | copy-start | bytes 9220
  199.3 10.2 copy-start.16
  209.1 1.4 copy-start.2
  230.5 11.6 %copy-start.4 = (f32[1024,768]{0,1:T(8,128)S(1)}, f32[1024,768]{0,1:T(8,128)}, u32[]{:S(2)}) copy-start(f32[1024,768]{0,1:T(8,128)} %copy-done.3) | copy-start | bytes 9437188
  243.8 1.6 copy-start.7
  249.3 445.7 %reduce-scatter.15.cloned.1.call-start = ((), (), s32[]{:S(2)}) async-start(), calls=%async_computation.12 | async-start | bytes 4423680 | tf_op jit(solution)/shard_map/reduce_scatter | solution.py:47
  271.6 0.7 copy-start
  294.9 17.5 %copy-start.1 = (bf16[1024,128]{0,1:T(8,128)(2,1)S(1)}, bf16[1024,128]{0,1:T(8,128)(2,1)}, u32[]{:S(2)}) copy-start(bf16[1024,128]{0,1:T(8,128)(2,1)} %copy.104) | copy-start | bytes 786436 | tf_op jit(solution)/shard_map/while
  330.9 0.7 copy-start
  354.2 17.5 %copy-start.1 = (bf16[1024,128]{0,1:T(8,128)(2,1)S(1)}, bf16[1024,128]{0,1:T(8,128)(2,1)}, u32[]{:S(2)}) copy-start(bf16[1024,128]{0,1:T(8,128)(2,1)} %copy.104) | copy-start | bytes 786436 | tf_op jit(solution)/shard_map/while
  390.3 0.7 copy-start
  413.6 17.5 %copy-start.1 = (bf16[1024,128]{0,1:T(8,128)(2,1)S(1)}, bf16[1024,128]{0,1:T(8,128)(2,1)}, u32[]{:S(2)}) copy-start(bf16[1024,128]{0,1:T(8,128)(2,1)} %copy.104) | copy-start | bytes 786436 | tf_op jit(solution)/shard_map/while
  449.7 0.7 copy-start
  472.9 17.4 %copy-start.1 = (bf16[1024,128]{0,1:T(8,128)(2,1)S(1)}, bf16[1024,128]{0,1:T(8,128)(2,1)}, u32[]{:S(2)}) copy-start(bf16[1024,128]{0,1:T(8,128)(2,1)} %copy.104) | copy-start | bytes 786436 | tf_op jit(solution)/shard_map/while
  509.0 0.7 copy-start
  532.3 17.5 %copy-start.1 = (bf16[1024,128]{0,1:T(8,128)(2,1)S(1)}, bf16[1024,128]{0,1:T(8,128)(2,1)}, u32[]{:S(2)}) copy-start(bf16[1024,128]{0,1:T(8,128)(2,1)} %copy.104) | copy-start | bytes 786436 | tf_op jit(solution)/shard_map/while
  568.4 0.7 copy-start
  591.6 17.5 %copy-start.1 = (bf16[1024,128]{0,1:T(8,128)(2,1)S(1)}, bf16[1024,128]{0,1:T(8,128)(2,1)}, u32[]{:S(2)}) copy-start(bf16[1024,128]{0,1:T(8,128)(2,1)} %copy.104) | copy-start | bytes 786436 | tf_op jit(solution)/shard_map/while
  616.2 3.7 copy-start.5
  619.6 1.7 copy-start.8
  619.7 2.6 copy-start.11
  620.3 1.5 copy-start.12
  628.8 153.9 %reduce-scatter.23.cloned.1.call-start = ((), (), s32[]{:S(2)}) async-start(), calls=%async_computation.16 | async-start | bytes 5898240 | tf_op jit(solution)/shard_map/reduce_scatter | solution.py:50
  638.5 0.7 copy-start.28
  638.5 232.4 %reduce-scatter.19.cloned.1.call-start = ((), (), s32[]{:S(2)}) async-start(), calls=%async_computation.14 | async-start | bytes 5898240 | tf_op jit(solution)/shard_map/reduce_scatter | solution.py:47
  649.1 286.6 %reduce-scatter.27.cloned.1.call-start = ((), (), s32[]{:S(2)}) async-start(), calls=%async_computation.18 | async-start | bytes 442368
  651.1 296.4 %reduce-scatter.25.cloned.1.call-start = ((), (), s32[]{:S(2)}) async-start(), calls=%async_computation.17 | async-start | bytes 1105920
  697.2 291.8 %reduce-scatter.29.cloned.1.call-start = ((), (), s32[]{:S(2)}) async-start(), calls=%async_computation.19 | async-start | bytes 1769472
  785.3 243.6 %reduce-scatter.21.cloned.1.call-start = ((), (), s32[]{:S(2)}) async-start(), calls=%async_computation.15 | async-start | bytes 1327104 | tf_op jit(solution)/shard_map/reduce_scatter | solution.py:55
  880.7 3.8 copy-start.23
  888.7 4.7 copy-start.15
  888.7 4.8 copy-start.17
  888.7 4.8 copy-start.21
  888.7 4.8 copy-start.22
Sparse Core Ops, SparseCore 0:
  26.3 35.5 all-gather.5
  64.4 23.9 all-gather.7
  90.2 38.8 all-gather.9
  130.8 39.6 all-gather.11
  249.4 28.7 reduce-scatter.16
  629.0 65.9 reduce-scatter.14
  697.3 85.4 reduce-scatter.22
  785.1 85.7 reduce-scatter.18
  874.0 34.3 reduce-scatter.26
  911.5 35.9 reduce-scatter.24
  950.7 38.3 reduce-scatter.28
  992.2 36.6 reduce-scatter.20
